TPU v7x, 256 devices: a whole 4x4x8 slice. The times are simulated.
256 devices in a mesh: dp: 32 (over z, y), section: 2 (over core), tensor: 4 (over x).
Axes of the slice: x: 4, y: 4, z: 8, core: 2. Of those that a mesh axis runs over, the one named last changes fastest.
Arguments:
- tokens: bfloat16 [8192, 2048], P('dp'), may hold values from -6 to 6
- base_rows: int32 [128], replicated, may hold values from 1 to 6, as said below
- baseline_owner: int32 [128], replicated, may hold values from 0 to 31, as said below
- cotangent: bfloat16 [2, 16384, 2048], P('section', 'dp'), may hold values from -6 to 6
- pre_gain: float32 [2, 2048], P('section'), may hold values from 0.25 to 1.75
- input_proj: bfloat16 [2, 2048, 2048], P('section', None, 'tensor'), may hold values from -0.125 to 0.125
- gate_proj: bfloat16 [2, 2048, 2048], P('section', None, 'tensor'), may hold values from -0.125 to 0.125
- state_proj: bfloat16 [2, 2048, 256], P('section'), may hold values from -0.125 to 0.125
- step_proj: bfloat16 [2, 2048, 32], P('section', None, 'tensor'), may hold values from -0.125 to 0.125
- step_bias: float32 [2, 32], P('section', 'tensor'), may hold values from -6 to -1.5
- decay_log: float32 [2, 32], P('section', 'tensor'), may hold values from 0 to 2.5
- skip_gain: float32 [2, 32], P('section', 'tensor'), may hold values from 0.5 to 1.5
- norm_gain: float32 [2, 2048], P('section', 'tensor'), may hold values from 0.25 to 1.75
- out_proj: bfloat16 [2, 2048, 2048], P('section', 'tensor'), may hold values from -0.125 to 0.125
Outputs:
- activations: bfloat16 [2, 16384, 2048], P('section', 'dp')
- out_grad: bfloat16 [2, 2048, 2048], P('section', 'tensor', 'dp')
Inputs may be any that keep to these rules, and one draw needn't show every extreme that they name: `base_rows`: over all baselines they sum to 256; some baseline has exactly 6. `baseline_owner`: every owner holds exactly 4 baselines; the base_rows of one owner's baselines sum to at most 16, and for some owner to exactly 16.
All inputs are finite; a program needn't handle non-finite values.
Results may differ from a plain program's by a relative error of at most 0.025.
Values may be sent and summed in bfloat16 or wider, within the bound.
A program may use at most 128 MiB of HBM per device.

v0:
```python
import jax
import jax.numpy as jnp
from jax import lax
from jax.sharding import PartitionSpec as P

HEADS = 32
HEADDIM = 64
NSTATE = 128
BLOCK = 64
MICRO = 2
EPS = 1e-05


def from_behind(value, axis, steps):
    count = lax.axis_size(axis)
    first, last = (max(0, -steps), min(count, count - steps))
    return lax.ppermute(value, axis, [(source, source + steps) for source in range(first, last)])


def layout_tables(base_rows, baseline_owner):
    count = base_rows.shape[0]
    index = jnp.arange(count, dtype=jnp.int32)
    ends = jnp.cumsum(base_rows)
    starts = ends - base_rows
    earlier = (baseline_owner[:, None] == baseline_owner[None, :]) & (
        index[None, :] < index[:, None]
    )
    owner_start = jnp.sum(jnp.where(earlier, base_rows[None, :], 0), axis=1)
    return (index, starts, ends, owner_start)


def block_scan(
    heads_in, b_rows, c_rows, step_size, decay_rate, segment, state, prev_segment, block
):
    total_rows, head_count, head_dim = heads_in.shape
    blocks = total_rows // block

    def advance(carried_in, item):
        state_now, segment_before = carried_in
        x_blk, b_blk, c_blk, dt_blk, seg_blk = item
        running = jnp.cumsum(dt_blk * decay_rate[None, :], axis=0)
        positions = jnp.arange(block, dtype=jnp.int32)
        together = (seg_blk[:, None] == seg_blk[None, :]) & (
            positions[:, None] >= positions[None, :]
        )
        spread = jnp.minimum(running[:, None, :] - running[None, :, :], 0.0)
        decay_mask = jnp.where(together[:, :, None], jnp.exp(spread), 0.0)
        scores = jnp.dot(c_blk, b_blk.T, preferred_element_type=jnp.float32)
        weights = (decay_mask * scores[:, :, None] * dt_blk[None, :, :]).astype(jnp.bfloat16)
        within = jnp.einsum("ijh,jhp->ihp", weights, x_blk, preferred_element_type=jnp.float32)
        keep_in = (seg_blk == segment_before).astype(jnp.float32)
        readout = jnp.einsum(
            "in,hpn->ihp", c_blk, state_now.astype(jnp.bfloat16), preferred_element_type=jnp.float32
        )
        from_state = keep_in[:, None, None] * jnp.exp(running)[:, :, None] * readout
        last_segment = seg_blk[-1]
        tail_weight = (
            jnp.where(
                (seg_blk == last_segment)[:, None], jnp.exp(running[-1][None, :] - running), 0.0
            )
            * dt_blk
        )
        scaled = (tail_weight[:, :, None] * x_blk.astype(jnp.float32)).astype(jnp.bfloat16)
        fresh_term = jnp.einsum("jhp,jn->hpn", scaled, b_blk, preferred_element_type=jnp.float32)
        keep_state = (last_segment == segment_before).astype(jnp.float32)
        state_next = keep_state * jnp.exp(running[-1])[:, None, None] * state_now + fresh_term
        return ((state_next, last_segment), within + from_state)

    scanned = (
        heads_in.reshape(blocks, block, head_count, head_dim),
        b_rows.reshape(blocks, block, -1),
        c_rows.reshape(blocks, block, -1),
        step_size.reshape(blocks, block, head_count),
        segment.reshape(blocks, block),
    )
    (state, prev_segment), outputs = lax.scan(advance, (state, prev_segment), scanned)
    return (outputs.reshape(total_rows, head_count, head_dim), state, prev_segment)


def block_layer(rows_in, segment, carried_state, params):
    (
        pre_gain,
        input_proj,
        gate_proj,
        state_proj,
        step_proj,
        step_bias,
        decay_log,
        skip_gain,
        norm_gain,
        out_proj,
    ) = params
    row_count = rows_in.shape[0]
    local_heads = step_proj.shape[1]
    rows_f = rows_in.astype(jnp.float32)
    normed = (
        rows_f * lax.rsqrt(jnp.mean(rows_f * rows_f, axis=-1, keepdims=True) + EPS) * pre_gain
    ).astype(jnp.bfloat16)
    scan_in = jax.nn.silu(jnp.dot(normed, input_proj, preferred_element_type=jnp.float32)).astype(
        jnp.bfloat16
    )
    gate_pre = jnp.dot(normed, gate_proj, preferred_element_type=jnp.float32)
    state_io = jax.nn.silu(jnp.dot(normed, state_proj, preferred_element_type=jnp.float32)).astype(
        jnp.bfloat16
    )
    step_size = jax.nn.softplus(
        jnp.dot(normed, step_proj, preferred_element_type=jnp.float32) + step_bias
    )
    decay_rate = -jnp.exp(decay_log)
    heads_in = scan_in.reshape(row_count, local_heads, HEADDIM)
    scan_out, state_end, segment_end = block_scan(
        heads_in,
        state_io[:, :NSTATE],
        state_io[:, NSTATE:],
        step_size,
        decay_rate,
        segment,
        carried_state[0],
        carried_state[1],
        BLOCK,
    )
    scan_out = scan_out + skip_gain[None, :, None] * heads_in.astype(jnp.float32)
    gated = scan_out.reshape(row_count, local_heads * HEADDIM) * jax.nn.silu(gate_pre)
    sq_sum = lax.psum(jnp.sum(gated * gated, axis=-1), "tensor")
    y_norm = (gated * lax.rsqrt(sq_sum[:, None] / (HEADS * HEADDIM) + EPS) * norm_gain).astype(
        jnp.bfloat16
    )
    row_share = row_count // lax.axis_size("tensor")
    summed = lax.psum_scatter(
        jnp.dot(y_norm, out_proj, preferred_element_type=jnp.float32).astype(jnp.bfloat16),
        "tensor",
        scatter_dimension=0,
        tiled=True,
    ).astype(jnp.float32)
    own_rows = lax.dynamic_slice_in_dim(rows_f, lax.axis_index("tensor") * row_share, row_share, 0)
    own_out = (own_rows + summed).astype(jnp.bfloat16)
    result = lax.all_gather(own_out, "tensor", axis=0, tiled=True)
    return (result, y_norm, (state_end, segment_end))


def grad_term(y_norm, cot_rows):
    return lax.dot_general(
        y_norm, cot_rows, (((0,), (0,)), ((), ())), preferred_element_type=jnp.float32
    )


def per_device(
    tokens,
    base_rows,
    baseline_owner,
    cotangent,
    pre_gain,
    input_proj,
    gate_proj,
    state_proj,
    step_proj,
    step_bias,
    decay_log,
    skip_gain,
    norm_gain,
    out_proj,
):
    dp_count = lax.axis_size("dp")
    tok_rows, feat_width = tokens.shape
    slot_cap = 2 * tok_rows // dp_count
    own_slots = slot_cap * dp_count
    index, starts, ends, owner_start = layout_tables(base_rows, baseline_owner)
    local = jnp.arange(tok_rows, dtype=jnp.int32)
    inside = ((starts[None, :] <= local[:, None]) & (local[:, None] < ends[None, :])).astype(
        jnp.int32
    )
    row_start = jnp.sum(inside * starts[None, :], axis=1)
    row_owner = jnp.sum(inside * baseline_owner[None, :], axis=1)
    row_ostart = jnp.sum(inside * owner_start[None, :], axis=1)
    send_slot = row_owner * slot_cap + row_ostart + local - row_start
    outgoing = (
        jnp.zeros((own_slots, feat_width), jnp.bfloat16)
        .at[send_slot]
        .set(tokens)
        .reshape(dp_count, slot_cap, feat_width)
    )
    owner_index = lax.axis_index("dp")
    place = jnp.arange(slot_cap, dtype=jnp.int32)
    held = (
        (baseline_owner[None, :] == owner_index)
        & (owner_start[None, :] <= place[:, None])
        & (place[:, None] < owner_start[None, :] + base_rows[None, :])
    ).astype(jnp.int32)
    got_start = jnp.sum(held * owner_start[None, :], axis=1)
    got_len = jnp.sum(held * base_rows[None, :], axis=1)
    got_id = jnp.sum(held * index[None, :], axis=1)
    got_any = jnp.sum(held, axis=1)
    sender = jnp.arange(dp_count, dtype=jnp.int32)[:, None]
    recv_slot = (
        dp_count * got_start[None, :]
        + sender * got_len[None, :]
        + place[None, :]
        - got_start[None, :]
    )
    recv_slot = jnp.where(got_any[None, :] > 0, recv_slot, own_slots).reshape(-1)
    id_rows = jnp.broadcast_to(got_id[None, :], (dp_count, slot_cap)).reshape(-1)
    slot_ids = jnp.full((own_slots,), -1, jnp.int32).at[recv_slot].set(id_rows, mode="drop")
    arrived = lax.all_to_all(outgoing, "dp", split_axis=0, concat_axis=0, tiled=True)
    width = arrived.shape[-1]
    stream = (
        jnp.zeros((own_slots, width), jnp.bfloat16)
        .at[recv_slot]
        .set(arrived.reshape(-1, width), mode="drop")
    )
    starts_flag = jnp.concatenate(
        [jnp.ones((1,), jnp.int32), (slot_ids[1:] != slot_ids[:-1]).astype(jnp.int32)]
    )
    segment = jnp.cumsum(starts_flag)
    section_idx = lax.axis_index("section")
    params = (
        pre_gain[0],
        input_proj[0],
        gate_proj[0],
        state_proj[0],
        step_proj[0],
        step_bias[0],
        decay_log[0],
        skip_gain[0],
        norm_gain[0],
        out_proj[0],
    )
    local_heads = step_proj.shape[2]
    micro_rows = own_slots // MICRO
    zero_state = (jnp.zeros((local_heads, HEADDIM, NSTATE), jnp.float32), jnp.array(-1, jnp.int32))
    cot_own = cotangent[0]
    carried_state = zero_state
    handed = jnp.zeros((micro_rows, feat_width), jnp.bfloat16)
    outputs_all = jnp.zeros((own_slots, feat_width), jnp.bfloat16)
    grad_acc = jnp.zeros((out_proj.shape[1], feat_width), jnp.float32)
    for turn_index in range(MICRO + 1):
        micro_index = turn_index - section_idx
        active_turn = (micro_index >= 0) & (micro_index < MICRO)
        micro_index = jnp.clip(micro_index, 0, MICRO - 1)
        first_row = micro_index * micro_rows
        own_in = lax.dynamic_slice_in_dim(stream, first_row, micro_rows, 0)
        source = jnp.where(section_idx == 0, own_in, handed)
        seg_part = lax.dynamic_slice_in_dim(segment, first_row, micro_rows, 0)
        result, y_norm, moved = block_layer(source, seg_part, carried_state, params)
        carried_state = jax.tree.map(
            lambda new_val, old_val: jnp.where(active_turn, new_val, old_val), moved, carried_state
        )
        outputs_all = jnp.where(
            active_turn,
            lax.dynamic_update_slice_in_dim(outputs_all, result, first_row, 0),
            outputs_all,
        )
        cot_part = lax.dynamic_slice_in_dim(cot_own, first_row, micro_rows, 0)
        grad_acc = grad_acc + jnp.where(active_turn, grad_term(y_norm, cot_part), 0.0)
        if turn_index < MICRO:
            handed = from_behind(result, "section", 1)
    grad_share = lax.psum_scatter(
        grad_acc.astype(jnp.bfloat16), "dp", scatter_dimension=1, tiled=True
    )
    return (outputs_all[None], grad_share[None])


def solution(mesh):
    return jax.shard_map(
        per_device,
        mesh=mesh,
        in_specs=(
            P("dp", None),
            P(),
            P(),
            P("section", "dp", None),
            P("section", None),
            P("section", None, "tensor"),
            P("section", None, "tensor"),
            P("section", None, None),
            P("section", None, "tensor"),
            P("section", "tensor"),
            P("section", "tensor"),
            P("section", "tensor"),
            P("section", "tensor"),
            P("section", "tensor", None),
        ),
        out_specs=(P("section", "dp", None), P("section", "tensor", "dp")),
        check_vma=False,
    )
```

profile of v0, /device:TPU:2, one launch (start us, length us, event | category | flops | bytes accessed | tf_op | source)
XLA Modules:
  0.0 645.6 jit_solution(3707332609720669846)
XLA Ops:
  10.8 4.4 scatter_custom_fusion
  15.2 11.8 %all-to-all-start = ((bf16[32,16,2048]{2,1,0:T(8,128)(2,1)}), bf16[32,16,2048]{2,1,0:T(8,128)(2,1)}, u32[]{:S(2)}, u32[]{:S(2)}) async-start(bf16[32,16,2048]{2,1,0:T(8,128)(2,1)} %bitcast.297), calls=%async_computation | async-start | bytes 4194304 | tf_op jit(solution)/shard_map/all_to_all | solution.py:203
  28.2 2.4 scatter_custom_fusion.2
  32.2 44.9 %all-to-all-done = bf16[32,16,2048]{2,1,0:T(8,128)(2,1)} async-done(((bf16[32,16,2048]{2,1,0:T(8,128)(2,1)}), bf16[32,16,2048]{2,1,0:T(8,128)(2,1)}, u32[]{:S(2)}, u32[]{:S(2)}) %all-to-all-start) | async-done | bytes 2097184 | tf_op jit(solution)/shard_map/all_to_all | solution.py:203
  77.1 6.1 scatter_custom_fusion.1
  83.2 1.6 multiply_reduce_fusion.2
  84.9 1.7 compare_select_fusion.2
  87.4 2.2 multiply_convert_fusion.20
  91.4 1.1 broadcast.415.clone2
  92.4 33.7 %while.45 = (s32[]{:T(128)}, f32[8,64,128]{2,1,0:T(8,128)S(1)}, s32[]{:T(128)}, f32[4,64,8,64]{3,2,1,0:T(8,128)}, s32[4,64]{1,0:T(4,128)S(1)}, /*index=5*/f32[4,...) while((s32[]{:T(128)}, f32[8,64,128]{2,1,0:T(8,128)S(1)}, ...), condition=%wide.region_17.18_spmd.clone, body=%wide.region_15.17_spmd.clone.sunk | while | flops 22689996 | bytes 2389582 | solution.py:76
  126.2 1.5 reshape.687
  127.7 2.9 multiply_reduce_fusion.5
  130.6 8.6 %psum.21 = f32[256]{0:T(256)S(1)} all-reduce(f32[256]{0:T(256)S(1)} %get-tuple-element.392), channel_id=1, replica_groups=mesh['dp'=32,'section'=2,'tensor'=4] {'tensor'}, use_global_device_ids=true, to_apply=%region_19.20 | all-reduce | flops 256 | bytes 2048 | tf_op jit(solution)/shard_map/psum | solution.py:124
  139.2 3.4 convolution_convert_fusion.2
  142.7 2.8 fusion.116
  145.5 18.4 %reduce-scatter.5.cloned.1.call-done = bf16[64,2048]{1,0:T(8,128)(2,1)} async-done(((bf16[256,2048]{1,0:T(8,128)(2,1)}), bf16[64,2048]{1,0:T(8,128)(2,1)}) %reduce-scatter.5.cloned.1.call-update) | async-done | bytes 262160 | tf_op jit(solution)/shard_map/reduce_scatter | solution.py:129
  163.9 1.9 add_convert_fusion.3
  165.9 27.4 %all-gather.4.cloned.1.call-done = bf16[256,2048]{1,0:T(8,128)(2,1)} async-done(((bf16[64,2048]{1,0:T(8,128)(2,1)}), bf16[256,2048]{1,0:T(8,128)(2,1)}) %all-gather.4.cloned.1.call-update) | async-done | bytes 1048592 | tf_op jit(solution)/shard_map/all_gather | solution.py:137
  193.3 2.3 collective-permute-start
  197.2 3.0 fusion.154
  204.4 1.1 reshape_reshape.10
  205.5 1.0 broadcast.415.clone2.1
  206.5 30.9 %while.43 = (s32[]{:T(128)}, f32[8,64,128]{2,1,0:T(8,128)S(1)}, s32[]{:T(128)}, f32[4,64,8,64]{3,2,1,0:T(8,128)}, s32[4,64]{1,0:T(4,128)}, /*index=5*/f32[4,64,8...) while((s32[]{:T(128)}, f32[8,64,128]{2,1,0:T(8,128)S(1)}, ...), condition=%wide.region_24.25_spmd, body=%wide.region_22.24_spmd.sunk | while | flops 22624460 | bytes 2581539 | solution.py:76
  237.4 2.3 reshape.692
  239.7 3.0 multiply_reduce_fusion.4
  242.8 9.2 %psum.22 = f32[256]{0:T(256)S(1)} all-reduce(f32[256]{0:T(256)S(1)} %get-tuple-element.394), channel_id=1, replica_groups=mesh['dp'=32,'section'=2,'tensor'=4] {'tensor'}, use_global_device_ids=true, to_apply=%region_26.27 | all-reduce | flops 256 | bytes 2048 | tf_op jit(solution)/shard_map/psum | solution.py:124
  252.0 3.3 convolution_convert_fusion.1
  255.4 24.6 %reduce-scatter.7.cloned.1.call-done = bf16[64,2048]{1,0:T(8,128)(2,1)} async-done(((bf16[256,2048]{1,0:T(8,128)(2,1)}), bf16[64,2048]{1,0:T(8,128)(2,1)}) %reduce-scatter.7.cloned.1.call-update) | async-done | bytes 262160 | tf_op jit(solution)/shard_map/reduce_scatter | solution.py:129
  280.0 1.9 add_convert_fusion.2
  282.0 27.4 %all-gather.6.cloned.1.call-done = bf16[256,2048]{1,0:T(8,128)(2,1)} async-done(((bf16[64,2048]{1,0:T(8,128)(2,1)}), bf16[256,2048]{1,0:T(8,128)(2,1)}) %all-gather.6.cloned.1.call-update) | async-done | bytes 1048592 | tf_op jit(solution)/shard_map/all_gather | solution.py:137
  309.4 2.3 collective-permute-start.1
  311.8 1.5 collective-permute-done.1
  313.3 3.0 fusion.153
  320.5 1.1 reshape_reshape.11
  321.6 1.0 broadcast.415.clone
  322.6 22.8 %while.44 = (s32[]{:T(128)}, f32[8,64,128]{2,1,0:T(8,128)S(1)}, s32[]{:T(128)}, f32[4,64,8,64]{3,2,1,0:T(8,128)}, s32[4,64]{1,0:T(4,128)S(1)}, /*index=5*/f32[4,...) while((s32[]{:T(128)}, f32[8,64,128]{2,1,0:T(8,128)S(1)}, ...), condition=%wide.region_31.32_spmd, body=%wide.region_29.31_spmd.sunk | while | flops 22624460 | bytes 2582019 | solution.py:76
  345.4 1.5 reshape.697
  346.9 2.8 multiply_reduce_fusion.3
  349.8 9.2 %psum.23 = f32[256]{0:T(256)S(1)} all-reduce(f32[256]{0:T(256)S(1)} %get-tuple-element.396), channel_id=1, replica_groups=mesh['dp'=32,'section'=2,'tensor'=4] {'tensor'}, use_global_device_ids=true, to_apply=%region_33.34 | all-reduce | flops 256 | bytes 2048 | tf_op jit(solution)/shard_map/psum | solution.py:124
  359.0 3.3 convolution_convert_fusion
  362.4 24.6 %reduce-scatter.9.cloned.1.call-done = bf16[64,2048]{1,0:T(8,128)(2,1)} async-done(((bf16[256,2048]{1,0:T(8,128)(2,1)}), bf16[64,2048]{1,0:T(8,128)(2,1)}) %reduce-scatter.9.cloned.1.call-update) | async-done | bytes 262160 | tf_op jit(solution)/shard_map/reduce_scatter | solution.py:129
  387.0 1.9 add_convert_fusion.1
  390.9 2.5 add_convert_fusion
  395.3 1.3 copy-done.1
  396.6 1.3 copy.198
  397.9 18.4 %all-gather.8.cloned.1.call-done = bf16[256,2048]{1,0:T(8,128)(2,1)} async-done(((bf16[64,2048]{1,0:T(8,128)(2,1)}), bf16[256,2048]{1,0:T(8,128)(2,1)}) %all-gather.8.cloned.1.call-update) | async-done | bytes 1048592 | tf_op jit(solution)/shard_map/all_gather | solution.py:137
  416.4 2.6 bitcast_dynamic-update-slice_fusion
  419.0 219.8 %reduce-scatter.11.cloned.1.call-done = bf16[512,64]{0,1:T(8,128)(2,1)} async-done(((bf16[512,2048]{0,1:T(8,128)(2,1)}), bf16[512,64]{0,1:T(8,128)(2,1)}) %reduce-scatter.11.cloned.1.call-update) | async-done | bytes 65552 | tf_op jit(solution)/shard_map/reduce_scatter | solution.py:256
  (423 shorter events, 94.5 us)
Async XLA Ops:
  7.2 381.8 %copy-start = (bf16[1,512,2048]{2,1,0:T(8,128)(2,1)S(1)}, bf16[1,512,2048]{2,1,0:T(8,128)(2,1)}, u32[]{:S(2)}) copy-start(bf16[1,512,2048]{2,1,0:T(8,128)(2,1)} %param.23) | copy-start | bytes 6291460
  15.2 11.9 %copy-start.26 = (f32[1,8]{1,0:T(1,128)S(1)}, f32[1,8]{1,0:T(1,128)}, u32[]{:S(2)}) copy-start(f32[1,8]{1,0:T(1,128)} %param.31) | copy-start | bytes 100
  15.2 12.6 %copy-start.20 = (s32[128]{0:T(128)S(1)}, s32[128]{0:T(128)}, u32[]{:S(2)}) copy-start(s32[128]{0:T(128)} %param.22) | copy-start | bytes 1540
  15.2 12.7 %copy-start.19 = (s32[128]{0:T(128)S(1)}, s32[128]{0:T(128)}, u32[]{:S(2)}) copy-start(s32[128]{0:T(128)} %param.21) | copy-start | bytes 1540
  15.2 17.0 %copy-start.38 = (f32[1,8]{1,0:T(1,128)S(1)}, f32[1,8]{1,0:T(1,128)}, u32[]{:S(2)}) copy-start(f32[1,8]{1,0:T(1,128)} %param.30) | copy-start | bytes 100
  15.2 61.9 %all-to-all-start = ((bf16[32,16,2048]{2,1,0:T(8,128)(2,1)}), bf16[32,16,2048]{2,1,0:T(8,128)(2,1)}, u32[]{:S(2)}, u32[]{:S(2)}) async-start(bf16[32,16,2048]{2,1,0:T(8,128)(2,1)} %bitcast.297), calls=%async_computation | async-start | bytes 4194304 | tf_op jit(solution)/shard_map/all_to_all | solution.py:203
  27.0 57.9 %copy-start.32 = (bf16[1,2048,8]{1,2,0:T(8,128)(2,1)S(1)}, bf16[1,2048,8]{1,2,0:T(8,128)(2,1)}, u32[]{:S(2)}) copy-start(bf16[1,2048,8]{1,2,0:T(8,128)(2,1)} %param.28) | copy-start | bytes 98308
  27.0 57.9 %copy-start.35 = (f32[1,2048]{1,0:T(1,128)S(1)}, f32[1,2048]{1,0:T(1,128)}, u32[]{:S(2)}) copy-start(f32[1,2048]{1,0:T(1,128)} %param.24) | copy-start | bytes 24580
  27.0 57.9 %copy-start.39 = (f32[1,8]{1,0:T(1,128)S(1)}, f32[1,8]{1,0:T(1,128)}, u32[]{:S(2)}) copy-start(f32[1,8]{1,0:T(1,128)} %param.29) | copy-start | bytes 100
  27.0 137.0 %reduce-scatter.5.cloned.1.call-start = ((), (), s32[]{:S(2)}) async-start(), calls=%async_computation.5 | async-start | bytes 1310720 | tf_op jit(solution)/shard_map/reduce_scatter | solution.py:129
  84.8 5.4 copy-start.24
  87.4 2.9 copy-start.2
  87.4 2.9 copy-start.27
  92.4 4.2 copy-start.17
  97.5 2.7 copy-start.18
  100.8 4.3 copy-start.17
  105.9 2.7 copy-start.18
  109.3 4.3 copy-start.17
  114.4 2.7 copy-start.18
  117.7 4.3 copy-start.17
  122.8 2.7 copy-start.18
  127.7 11.6 %copy-start.11 = (f32[1,512]{1,0:T(1,128)S(1)}, f32[1,512]{1,0:T(1,128)}, u32[]{:S(2)}) copy-start(f32[1,512]{1,0:T(1,128)} %param.32) | copy-start | bytes 6148
  130.5 12.0 %copy-start.5 = (f32[256,512]{1,0:T(8,128)}, f32[256,512]{1,0:T(8,128)S(1)}, u32[]{:S(2)}) copy-start(f32[256,512]{1,0:T(8,128)S(1)} %get-tuple-element.393) | copy-start | bytes 1572868
  139.2 3.4 copy-start.15
  142.6 50.7 %all-gather.4.cloned.1.call-start = ((), (), s32[]{:S(2)}) async-start(), calls=%async_computation.6 | async-start | bytes 1310720 | tf_op jit(solution)/shard_map/all_gather | solution.py:137
  142.7 52.9 %copy-start.22 = (s32[256]{0:T(256)S(1)}, s32[256]{0:T(256)}, u32[]{:S(2)}) copy-start(s32[256]{0:T(256)} %get-tuple-element.388) | copy-start | bytes 3076
  165.9 114.2 %reduce-scatter.7.cloned.1.call-start = ((), (), s32[]{:S(2)}) async-start(), calls=%async_computation.7 | async-start | bytes 1310720 | tf_op jit(solution)/shard_map/reduce_scatter | solution.py:129
  193.3 3.9 collective-permute-start
  196.3 4.3 copy-start.33
  196.3 4.3 copy-start.36
  196.3 4.3 copy-start.40
  200.2 2.2 copy-start.4
  204.2 2.3 copy-start.13
  242.8 12.6 %copy-start.7 = (f32[256,512]{1,0:T(8,128)}, f32[256,512]{1,0:T(8,128)S(1)}, u32[]{:S(2)}) copy-start(f32[256,512]{1,0:T(8,128)S(1)} %get-tuple-element.395) | copy-start | bytes 1572868
  255.3 56.3 %copy-start.21 = (s32[256]{0:T(256)S(1)}, s32[256]{0:T(256)}, u32[]{:S(2)}) copy-start(s32[256]{0:T(256)} %get-tuple-element.387) | copy-start | bytes 3076
  255.4 54.0 %all-gather.6.cloned.1.call-start = ((), (), s32[]{:S(2)}) async-start(), calls=%async_computation.8 | async-start | bytes 1310720 | tf_op jit(solution)/shard_map/all_gather | solution.py:137
  281.9 105.1 %reduce-scatter.9.cloned.1.call-start = ((), (), s32[]{:S(2)}) async-start(), calls=%async_computation.9 | async-start | bytes 1310720 | tf_op jit(solution)/shard_map/reduce_scatter | solution.py:129
  309.4 3.9 collective-permute-start.1
  311.8 4.8 copy-start.34
  311.8 4.8 copy-start.37
  311.8 4.8 copy-start.41
  316.3 2.2 copy-start.3
  320.3 2.3 copy-start.12
  322.6 24.3 %copy-start.23 = (f32[512]{0:T(512)S(1)}, f32[512]{0:T(512)}, u32[]{:S(2)}) copy-start(f32[512]{0:T(512)} %mul.547) | copy-start | bytes 6148
  362.3 26.7 %copy-start.6 = (f32[256,512]{1,0:T(8,128)S(1)}, f32[256,512]{1,0:T(8,128)}, u32[]{:S(2)}) copy-start(f32[256,512]{1,0:T(8,128)} %copy-done.5) | copy-start | bytes 1572868
  362.3 26.7 %copy-start.16 = (f32[256]{0:T(256)S(1)}, f32[256]{0:T(256)}, u32[]{:S(2)}) copy-start(f32[256]{0:T(256)} %copy-done.15) | copy-start | bytes 3076
  362.3 54.0 %all-gather.8.cloned.1.call-start = ((), (), s32[]{:S(2)}) async-start(), calls=%async_computation.10 | async-start | bytes 1310720 | tf_op jit(solution)/shard_map/all_gather | solution.py:137
  388.9 249.8 %reduce-scatter.11.cloned.1.call-start = ((), (), s32[]{:S(2)}) async-start(), calls=%async_computation.11 | async-start | bytes 2162688 | tf_op jit(solution)/shard_map/reduce_scatter | solution.py:256
  (10 other events, 14.7 us)
Sparse Core Ops, SparseCore 0:
  142.7 21.1 reduce-scatter.4
  166.0 27.2 all-gather.3
  255.5 24.5 reduce-scatter.6
  282.0 27.2 all-gather.5
  362.5 24.5 reduce-scatter.8
  389.1 27.2 all-gather.7
  421.2 217.4 reduce-scatter.10
where the time goes:
time: 648 us; the launch traced here: 646 us
  waiting for transfers between devices  408 us (63%)
  local copies, waits for them, and re-layouts  66.8 us (10%)
  matrix products  51.8 us (8%)
  other arithmetic  44.7 us (7%)
  blocking collectives  27 us (4%)
  starting transfers between devices  16.6 us (3%)
  loops' own time  15.7 us (2%)
  between operations  14.8 us (2%)
    reduce_scatter x1, waiting for transfers between devices, per_device(): lax.psum_scatter(grad_acc.astype(jnp.bfloat16), 'dp', scatter_dimension=1...  220 us
    all_gather x3, waiting for transfers between devices, block_layer(): result = lax.all_gather(own_out, 'tensor', axis=0, tiled=True)  73.3 us
    reduce_scatter x3, waiting for transfers between devices, block_layer(): lax.psum_scatter(jnp.dot(y_norm, out_proj, preferred_element_type=jnp.flo...  67.7 us
    all_to_all x1, waiting for transfers between devices, per_device(): lax.all_to_all(outgoing, 'dp', split_axis=0, concat_axis=0, tiled=True)  44.9 us
    psum x3, blocking collectives, block_layer(): sq_sum = lax.psum(jnp.sum(gated * gated, axis=-1), 'tensor')  27 us
    another operation x3, loops' own time, block_scan(): lax.scan(advance, (state, prev_segment), scanned)  15.7 us
  transfers between devices with their start and end apart: 10, of which 10 were waited for; matrix products, arithmetic and copies ran while one was open for 3% of the time, Pallas kernels for 0%

commit v1 on v0

--- a/solution.py
+++ b/solution.py
@@ -9,6 +9,19 @@
 BLOCK = 64
 MICRO = 2
 EPS = 1e-05
+
+
+def handle_sums_all(arr_in):
+    parts_n = lax.psum(1, "tensor")
+    samples = list(map(lambda p: (p, (p + 1) % parts_n), range(parts_n)))
+    table = list(map(lambda p: (p, (p - 1) % parts_n), range(parts_n)))
+    upper, arr_out = ([arr_in], [arr_in])
+    for _ in range(parts_n // 2):
+        upper.append(lax.ppermute(upper[-1], "tensor", samples))
+    for _ in tuple(range((parts_n - 1) // 2)):
+        arr_out.append(lax.ppermute(arr_out[-1], "tensor", table))
+    response = jnp.concatenate([*upper[::-1], *arr_out[1:]], axis=0)
+    return jnp.roll(response, (lax.axis_index("tensor") - parts_n // 2) * arr_in.shape[0], axis=0)
 
 
 def from_behind(value, axis, steps):
@@ -134,7 +147,7 @@
     ).astype(jnp.float32)
     own_rows = lax.dynamic_slice_in_dim(rows_f, lax.axis_index("tensor") * row_share, row_share, 0)
     own_out = (own_rows + summed).astype(jnp.bfloat16)
-    result = lax.all_gather(own_out, "tensor", axis=0, tiled=True)
+    result = handle_sums_all(own_out)
     return (result, y_norm, (state_end, segment_end))
 
 

time: 648 us -> 618 us (0.954); the launches traced: 646 us -> 609 us
  waiting for transfers between devices: 408 us -> 340 us
  other arithmetic: 44.7 us -> 56.7 us
  starting transfers between devices: 16.6 us -> 28.3 us
    all_gather x3 -> x0, waiting for transfers between devices: 73.3 us -> none  [block_layer(): result = lax.all_gather(own_out, 'tensor', axis=0, tiled=True)]
    ppermute x0 -> x9, waiting for transfers between devices: none -> 30.1 us  [the longest x6 30.1 us: handle_sums_all(): upper.append(lax.ppermute(upper[-1], 'tensor', samples))]
    reduce_scatter x1, waiting for transfers between devices: 220 us -> 201 us  [per_device(): lax.psum_scatter(grad_acc.astype(jnp.bfloat16), 'dp', scatter_dimension=1...]
    select_n x3, other arithmetic: 3.22 us -> 16.4 us  [per_device(): jnp.where(active_turn, lax.dynamic_update_slice_in_dim(outputs_all, resul...]
    ppermute x0 -> x9, starting transfers between devices: none -> 11.5 us  [the longest x6 9.4 us: handle_sums_all(): upper.append(lax.ppermute(upper[-1], 'tensor', samples))]
  transfers between devices with their start and end apart: 10 -> 16, of which waited for: 10 -> 13; matrix products, arithmetic and copies ran while one was open for 3% -> 4% of each run, Pallas kernels for 0% -> 0%
where the time goes in v1:
time: 618 us; the launch traced here: 609 us
  waiting for transfers between devices  340 us (55%)
  local copies, waits for them, and re-layouts  68.7 us (11%)
  other arithmetic  56.7 us (9%)
  matrix products  52 us (8%)
  blocking collectives  30.6 us (5%)
  starting transfers between devices  28.3 us (5%)
  loops' own time  17.3 us (3%)
  between operations  14.8 us (2%)
    reduce_scatter x1, waiting for transfers between devices, per_device(): lax.psum_scatter(grad_acc.astype(jnp.bfloat16), 'dp', scatter_dimension=1...  201 us
    reduce_scatter x3, waiting for transfers between devices, block_layer(): lax.psum_scatter(jnp.dot(y_norm, out_proj, preferred_element_type=jnp.flo...  62.2 us
    all_to_all x1, waiting for transfers between devices, per_device(): lax.all_to_all(outgoing, 'dp', split_axis=0, concat_axis=0, tiled=True)  44.9 us
    psum x3, blocking collectives, block_layer(): sq_sum = lax.psum(jnp.sum(gated * gated, axis=-1), 'tensor')  30.6 us
    ppermute x6, waiting for transfers between devices, handle_sums_all(): upper.append(lax.ppermute(upper[-1], 'tensor', samples))  30.1 us
    another operation x3, loops' own time, block_scan(): lax.scan(advance, (state, prev_segment), scanned)  17.3 us
    select_n x3, other arithmetic, per_device(): jnp.where(active_turn, lax.dynamic_update_slice_in_dim(outputs_all, resul...  16.4 us
  transfers between devices with their start and end apart: 16, of which 13 were waited for; matrix products, arithmetic and copies ran while one was open for 4% of the time, Pallas kernels for 0%

profile of v1, /device:TPU:2, one launch (start us, length us, event | category | flops | bytes accessed | tf_op | source)
XLA Modules:
  0.0 608.6 jit_solution(11130930109815143018)
XLA Ops:
  10.8 4.4 scatter_custom_fusion
  15.2 11.8 %all-to-all-start = ((bf16[32,16,2048]{2,1,0:T(8,128)(2,1)}), bf16[32,16,2048]{2,1,0:T(8,128)(2,1)}, u32[]{:S(2)}, u32[]{:S(2)}) async-start(bf16[32,16,2048]{2,1,0:T(8,128)(2,1)} %bitcast.298), calls=%async_computation | async-start | bytes 4194304 | tf_op jit(solution)/shard_map/all_to_all | solution.py:216
  28.2 2.4 scatter_custom_fusion.2
  32.2 44.9 %all-to-all-done = bf16[32,16,2048]{2,1,0:T(8,128)(2,1)} async-done(((bf16[32,16,2048]{2,1,0:T(8,128)(2,1)}), bf16[32,16,2048]{2,1,0:T(8,128)(2,1)}, u32[]{:S(2)}, u32[]{:S(2)}) %all-to-all-start) | async-done | bytes 2097184 | tf_op jit(solution)/shard_map/all_to_all | solution.py:216
  77.1 6.6 %scatter_custom_fusion.1 = bf16[512,2048]{1,0:T(8,128)(2,1)} fusion(s32[512]{0:T(512)S(1)} %bitcast.318, bf16[512,2048]{1,0:T(8,128)(2,1)} %bitcast.30, bf16[]{:T(256)} %constant.141.clone.1), kind=kCustom, calls=%fused_computation.230 | custom fusion | bytes 2097664 | tf_op jit(solution)/shard_map/scatter | solution.py:221
  83.7 1.6 multiply_reduce_fusion.2
  85.4 1.7 compare_select_fusion.2
  87.9 2.2 multiply_convert_fusion.20
  92.9 34.9 %while.45 = (s32[]{:T(128)}, f32[8,64,128]{2,1,0:T(8,128)S(1)}, s32[]{:T(128)}, f32[4,64,8,64]{3,2,1,0:T(8,128)}, s32[4,64]{1,0:T(4,128)S(1)}, /*index=5*/f32[4,...) while((s32[]{:T(128)}, f32[8,64,128]{2,1,0:T(8,128)S(1)}, ...), condition=%wide.region_17.18_spmd.clone, body=%wide.region_15.17_spmd.clone.sunk | while | flops 22689996 | bytes 2389582 | solution.py:89
  127.8 1.5 reshape.687
  129.3 2.9 multiply_reduce_fusion.5
  132.2 8.6 %psum.21 = f32[256]{0:T(256)S(1)} all-reduce(f32[256]{0:T(256)S(1)} %get-tuple-element.397), channel_id=1, replica_groups=mesh['dp'=32,'section'=2,'tensor'=4] {'tensor'}, use_global_device_ids=true, to_apply=%region_19.20 | all-reduce | flops 256 | bytes 2048 | tf_op jit(solution)/shard_map/psum | solution.py:137
  140.9 3.4 convolution_convert_fusion.2
  144.3 2.8 fusion.140
  147.1 18.5 %reduce-scatter.5.cloned.1.call-done = bf16[64,2048]{1,0:T(8,128)(2,1)} async-done(((bf16[256,2048]{1,0:T(8,128)(2,1)}), bf16[64,2048]{1,0:T(8,128)(2,1)}) %reduce-scatter.5.cloned.1.call-update) | async-done | bytes 262160 | tf_op jit(solution)/shard_map/reduce_scatter | solution.py:142
  166.8 1.9 collective-permute-start
  169.4 4.9 collective-permute-done
  175.4 6.2 %collective-permute-done.1 = bf16[64,2048]{1,0:T(8,128)(2,1)S(1)} collective-permute-done((bf16[64,2048]{1,0:T(8,128)(2,1)S(1)}, bf16[64,2048]{1,0:T(8,128)(2,1)S(1)}, u32[]{:S(2)}, u32[]{:S(2)}) %collective-permute-start.1) | collective-permute-done | bytes 262176 | tf_op jit(solution)/shard_map/ppermute | solution.py:20
  181.6 1.6 broadcast.410
  183.2 4.7 select_dynamic-update-slice_fusion.1
  187.9 2.4 collective-permute-start.3
  191.8 3.0 fusion.179
  201.1 31.3 %while.43 = (s32[]{:T(128)}, f32[8,64,128]{2,1,0:T(8,128)S(1)}, s32[]{:T(128)}, f32[4,64,8,64]{3,2,1,0:T(8,128)}, s32[4,64]{1,0:T(4,128)}, /*index=5*/f32[4,64,8...) while((s32[]{:T(128)}, f32[8,64,128]{2,1,0:T(8,128)S(1)}, ...), condition=%wide.region_24.26_spmd, body=%wide.region_22.25_spmd.sunk | while | flops 22624460 | bytes 2581539 | solution.py:89
  232.4 2.3 reshape.692
  234.7 3.0 multiply_reduce_fusion.4
  237.7 11.0 %psum.22 = f32[256]{0:T(256)S(1)} all-reduce(f32[256]{0:T(256)S(1)} %get-tuple-element.399), channel_id=1, replica_groups=mesh['dp'=32,'section'=2,'tensor'=4] {'tensor'}, use_global_device_ids=true, to_apply=%region_26.28 | all-reduce | flops 256 | bytes 2048 | tf_op jit(solution)/shard_map/psum | solution.py:137
  248.7 3.4 convolution_convert_fusion.1
  252.2 23.9 %reduce-scatter.7.cloned.1.call-done = bf16[64,2048]{1,0:T(8,128)(2,1)} async-done(((bf16[256,2048]{1,0:T(8,128)(2,1)}), bf16[64,2048]{1,0:T(8,128)(2,1)}) %reduce-scatter.7.cloned.1.call-update) | async-done | bytes 262160 | tf_op jit(solution)/shard_map/reduce_scatter | solution.py:142
  277.3 2.0 collective-permute-start.4
  280.0 4.9 collective-permute-done.4
  286.0 6.3 %collective-permute-done.5 = bf16[64,2048]{1,0:T(8,128)(2,1)} collective-permute-done((bf16[64,2048]{1,0:T(8,128)(2,1)S(1)}, bf16[64,2048]{1,0:T(8,128)(2,1)}, u32[]{:S(2)}, u32[]{:S(2)}) %collective-permute-start.5) | collective-permute-done | bytes 262176 | tf_op jit(solution)/shard_map/ppermute | solution.py:20
  292.3 5.9 select_dynamic-update-slice_fusion
  298.2 2.5 collective-permute-start.7
  302.1 3.0 fusion.177
  311.4 24.7 %while.44 = (s32[]{:T(128)}, f32[8,64,128]{2,1,0:T(8,128)S(1)}, s32[]{:T(128)}, f32[4,64,8,64]{3,2,1,0:T(8,128)}, s32[4,64]{1,0:T(4,128)S(1)}, /*index=5*/f32[4,...) while((s32[]{:T(128)}, f32[8,64,128]{2,1,0:T(8,128)S(1)}, ...), condition=%wide.region_31.33_spmd, body=%wide.region_29.32_spmd.sunk | while | flops 22624460 | bytes 2590267 | solution.py:89
  336.1 1.5 reshape.697
  337.6 2.8 multiply_reduce_fusion.3
  340.5 11.0 %psum.23 = f32[256]{0:T(256)S(1)} all-reduce(f32[256]{0:T(256)S(1)} %get-tuple-element.401), channel_id=1, replica_groups=mesh['dp'=32,'section'=2,'tensor'=4] {'tensor'}, use_global_device_ids=true, to_apply=%region_33.35 | all-reduce | flops 256 | bytes 2048 | tf_op jit(solution)/shard_map/psum | solution.py:137
  351.5 3.4 convolution_convert_fusion
  356.8 2.4 add_convert_fusion
  359.3 19.7 %reduce-scatter.9.cloned.1.call-done = bf16[64,2048]{1,0:T(8,128)(2,1)} async-done(((bf16[256,2048]{1,0:T(8,128)(2,1)}), bf16[64,2048]{1,0:T(8,128)(2,1)}) %reduce-scatter.9.cloned.1.call-update) | async-done | bytes 262160 | tf_op jit(solution)/shard_map/reduce_scatter | solution.py:142
  380.1 1.9 collective-permute-start.8
  382.8 4.9 collective-permute-done.8
  387.6 1.3 collective-permute-start.9
  389.0 3.2 copy.198
  392.1 3.0 collective-permute-done.9
  395.2 5.7 fusion.104
  400.9 200.9 %reduce-scatter.11.cloned.1.call-done = bf16[512,64]{0,1:T(8,128)(2,1)} async-done(((bf16[512,2048]{0,1:T(8,128)(2,1)}), bf16[512,64]{0,1:T(8,128)(2,1)}) %reduce-scatter.11.cloned.1.call-update) | async-done | bytes 65552 | tf_op jit(solution)/shard_map/reduce_scatter | solution.py:269
  (452 shorter events, 108.6 us)
Async XLA Ops:
  7.2 347.8 %copy-start = (bf16[1,512,2048]{2,1,0:T(8,128)(2,1)S(1)}, bf16[1,512,2048]{2,1,0:T(8,128)(2,1)}, u32[]{:S(2)}) copy-start(bf16[1,512,2048]{2,1,0:T(8,128)(2,1)} %param.25) | copy-start | bytes 6291460
  15.2 11.9 %copy-start.29 = (f32[1,8]{1,0:T(1,128)S(1)}, f32[1,8]{1,0:T(1,128)}, u32[]{:S(2)}) copy-start(f32[1,8]{1,0:T(1,128)} %param.33) | copy-start | bytes 100
  15.2 12.6 %copy-start.21 = (s32[128]{0:T(128)S(1)}, s32[128]{0:T(128)}, u32[]{:S(2)}) copy-start(s32[128]{0:T(128)} %param.24) | copy-start | bytes 1540
  15.2 12.6 %copy-start.20 = (s32[128]{0:T(128)S(1)}, s32[128]{0:T(128)}, u32[]{:S(2)}) copy-start(s32[128]{0:T(128)} %param.23) | copy-start | bytes 1540
  15.2 17.0 %copy-start.42 = (f32[1,8]{1,0:T(1,128)S(1)}, f32[1,8]{1,0:T(1,128)}, u32[]{:S(2)}) copy-start(f32[1,8]{1,0:T(1,128)} %param.32) | copy-start | bytes 100
  15.2 61.9 %all-to-all-start = ((bf16[32,16,2048]{2,1,0:T(8,128)(2,1)}), bf16[32,16,2048]{2,1,0:T(8,128)(2,1)}, u32[]{:S(2)}, u32[]{:S(2)}) async-start(bf16[32,16,2048]{2,1,0:T(8,128)(2,1)} %bitcast.298), calls=%async_computation | async-start | bytes 4194304 | tf_op jit(solution)/shard_map/all_to_all | solution.py:216
  27.0 58.4 %copy-start.35 = (bf16[1,2048,8]{1,2,0:T(8,128)(2,1)S(1)}, bf16[1,2048,8]{1,2,0:T(8,128)(2,1)}, u32[]{:S(2)}) copy-start(bf16[1,2048,8]{1,2,0:T(8,128)(2,1)} %param.30) | copy-start | bytes 98308
  27.0 58.4 %copy-start.38 = (f32[1,2048]{1,0:T(1,128)S(1)}, f32[1,2048]{1,0:T(1,128)}, u32[]{:S(2)}) copy-start(f32[1,2048]{1,0:T(1,128)} %param.26) | copy-start | bytes 24580
  27.0 58.4 %copy-start.43 = (f32[1,8]{1,0:T(1,128)S(1)}, f32[1,8]{1,0:T(1,128)}, u32[]{:S(2)}) copy-start(f32[1,8]{1,0:T(1,128)} %param.31) | copy-start | bytes 100
  27.0 138.6 %reduce-scatter.5.cloned.1.call-start = ((), (), s32[]{:S(2)}) async-start(), calls=%async_computation.5 | async-start | bytes 1310720 | tf_op jit(solution)/shard_map/reduce_scatter | solution.py:142
  85.3 5.4 copy-start.27
  87.9 2.9 copy-start.30
  92.9 4.5 copy-start.18
  101.6 4.5 copy-start.18
  110.4 4.5 copy-start.18
  119.1 4.5 copy-start.18
  129.3 11.6 %copy-start.8 = (f32[1,512]{1,0:T(1,128)S(1)}, f32[1,512]{1,0:T(1,128)}, u32[]{:S(2)}) copy-start(f32[1,512]{1,0:T(1,128)} %param.34) | copy-start | bytes 6148
  132.2 12.1 %copy-start.4 = (f32[256,512]{1,0:T(8,128)}, f32[256,512]{1,0:T(8,128)S(1)}, u32[]{:S(2)}) copy-start(f32[256,512]{1,0:T(8,128)S(1)} %get-tuple-element.398) | copy-start | bytes 1572868
  140.9 3.4 copy-start.12
  144.3 131.8 %reduce-scatter.7.cloned.1.call-start = ((), (), s32[]{:S(2)}) async-start(), calls=%async_computation.6 | async-start | bytes 1310720 | tf_op jit(solution)/shard_map/reduce_scatter | solution.py:142
  166.8 7.5 %collective-permute-start = (bf16[64,2048]{1,0:T(8,128)(2,1)S(1)}, bf16[64,2048]{1,0:T(8,128)(2,1)S(1)}, u32[]{:S(2)}, u32[]{:S(2)}) collective-permute-start(bf16[64,2048]{1,0:T(8,128)(2,1)S(1)} %add_convert_fusion.3), channel_id=1, source_target_pairs={{0,1},{1,2},{2,3},{3,0},{4,5},{5,6},{6,7},{7,4},{8,9},{9,10},{10,1... | collective-permute-start | bytes 786440 | tf_op jit(solution)/shard_map/ppermute | solution.py:20
  168.7 6.7 %collective-permute-start.2 = (bf16[64,2048]{1,0:T(8,128)(2,1)S(1)}, bf16[64,2048]{1,0:T(8,128)(2,1)S(1)}, u32[]{:S(2)}, u32[]{:S(2)}) collective-permute-start(bf16[64,2048]{1,0:T(8,128)(2,1)S(1)} %add_convert_fusion.3), channel_id=1, source_target_pairs={{0,3},{1,0},{2,1},{3,2},{4,7},{5,4},{6,5},{7,6},{8,11},{9,8},{10,9... | collective-permute-start | bytes 786440 | tf_op jit(solution)/shard_map/ppermute | solution.py:22
  174.3 7.3 %collective-permute-start.1 = (bf16[64,2048]{1,0:T(8,128)(2,1)S(1)}, bf16[64,2048]{1,0:T(8,128)(2,1)S(1)}, u32[]{:S(2)}, u32[]{:S(2)}) collective-permute-start(bf16[64,2048]{1,0:T(8,128)(2,1)S(1)} %collective-permute-done), channel_id=1, source_target_pairs={{0,1},{1,2},{2,3},{3,0},{4,5},{5,6},{6,7},{7,4},{8,9},{9,10},{10,1... | collective-permute-start | bytes 786440 | tf_op jit(solution)/shard_map/ppermute | solution.py:20
  183.2 7.1 %copy-start.23 = (s32[256]{0:T(256)S(1)}, s32[256]{0:T(256)}, u32[]{:S(2)}) copy-start(s32[256]{0:T(256)} %get-tuple-element.393) | copy-start | bytes 3076
  187.9 3.9 collective-permute-start.3
  191.0 4.1 copy-start.36
  191.0 4.1 copy-start.39
  191.0 4.1 copy-start.44
  237.7 14.4 %copy-start.6 = (f32[256,512]{1,0:T(8,128)}, f32[256,512]{1,0:T(8,128)S(1)}, u32[]{:S(2)}) copy-start(f32[256,512]{1,0:T(8,128)S(1)} %get-tuple-element.400) | copy-start | bytes 1572868
  248.7 3.4 copy-start.14
  252.1 126.8 %reduce-scatter.9.cloned.1.call-start = ((), (), s32[]{:S(2)}) async-start(), calls=%async_computation.7 | async-start | bytes 1310720 | tf_op jit(solution)/shard_map/reduce_scatter | solution.py:142
  277.3 7.6 %collective-permute-start.4 = (bf16[64,2048]{1,0:T(8,128)(2,1)S(1)}, bf16[64,2048]{1,0:T(8,128)(2,1)S(1)}, u32[]{:S(2)}, u32[]{:S(2)}) collective-permute-start(bf16[64,2048]{1,0:T(8,128)(2,1)S(1)} %add_convert_fusion.2), channel_id=1, source_target_pairs={{0,1},{1,2},{2,3},{3,0},{4,5},{5,6},{6,7},{7,4},{8,9},{9,10},{10,1... | collective-permute-start | bytes 786440 | tf_op jit(solution)/shard_map/ppermute | solution.py:20
  279.3 6.7 %collective-permute-start.6 = (bf16[64,2048]{1,0:T(8,128)(2,1)S(1)}, bf16[64,2048]{1,0:T(8,128)(2,1)S(1)}, u32[]{:S(2)}, u32[]{:S(2)}) collective-permute-start(bf16[64,2048]{1,0:T(8,128)(2,1)S(1)} %add_convert_fusion.2), channel_id=1, source_target_pairs={{0,3},{1,0},{2,1},{3,2},{4,7},{5,4},{6,5},{7,6},{8,11},{9,8},{10,9... | collective-permute-start | bytes 786440 | tf_op jit(solution)/shard_map/ppermute | solution.py:22
  284.8 7.4 %collective-permute-start.5 = (bf16[64,2048]{1,0:T(8,128)(2,1)S(1)}, bf16[64,2048]{1,0:T(8,128)(2,1)}, u32[]{:S(2)}, u32[]{:S(2)}) collective-permute-start(bf16[64,2048]{1,0:T(8,128)(2,1)S(1)} %collective-permute-done.4), channel_id=1, source_target_pairs={{0,1},{1,2},{2,3},{3,0},{4,5},{5,6},{6,7},{7,4},{8,9},{9,10},{10,1... | collective-permute-start | bytes 786440 | tf_op jit(solution)/shard_map/ppermute | solution.py:20
  292.3 8.4 %copy-start.22 = (s32[256]{0:T(256)S(1)}, s32[256]{0:T(256)}, u32[]{:S(2)}) copy-start(s32[256]{0:T(256)} %get-tuple-element.392) | copy-start | bytes 3076
  298.2 3.9 collective-permute-start.7
  300.8 4.6 copy-start.37
  300.8 4.6 copy-start.40
  300.8 4.6 copy-start.45
  311.4 26.2 %copy-start.24 = (f32[512]{0:T(512)S(1)}, f32[512]{0:T(512)}, u32[]{:S(2)}) copy-start(f32[512]{0:T(512)} %mul.552) | copy-start | bytes 6148
  311.4 26.2 %copy-start.26 = (f32[256]{0:T(256)S(1)}, f32[256]{0:T(256)}, u32[]{:S(2)}) copy-start(f32[256]{0:T(256)} %copy-done.25) | copy-start | bytes 3076
  311.4 26.2 %copy-start.41 = (f32[1,2048]{1,0:T(1,128)S(1)}, f32[1,2048]{1,0:T(1,128)}, u32[]{:S(2)}) copy-start(f32[1,2048]{1,0:T(1,128)} %param.26) | copy-start | bytes 24580
  351.5 3.5 copy-start.5
  351.5 3.5 copy-start.13
  354.9 246.9 %reduce-scatter.11.cloned.1.call-start = ((), (), s32[]{:S(2)}) async-start(), calls=%async_computation.8 | async-start | bytes 2162688 | tf_op jit(solution)/shard_map/reduce_scatter | solution.py:269
  380.1 7.5 %collective-permute-start.8 = (bf16[64,2048]{1,0:T(8,128)(2,1)S(1)}, bf16[64,2048]{1,0:T(8,128)(2,1)S(1)}, u32[]{:S(2)}, u32[]{:S(2)}) collective-permute-start(bf16[64,2048]{1,0:T(8,128)(2,1)S(1)} %add_convert_fusion.1), channel_id=1, source_target_pairs={{0,1},{1,2},{2,3},{3,0},{4,5},{5,6},{6,7},{7,4},{8,9},{9,10},{10,1... | collective-permute-start | bytes 786440 | tf_op jit(solution)/shard_map/ppermute | solution.py:20
  382.0 10.1 %collective-permute-start.10 = (bf16[64,2048]{1,0:T(8,128)(2,1)S(1)}, bf16[64,2048]{1,0:T(8,128)(2,1)S(1)}, u32[]{:S(2)}, u32[]{:S(2)}) collective-permute-start(bf16[64,2048]{1,0:T(8,128)(2,1)S(1)} %add_convert_fusion.1), channel_id=1, source_target_pairs={{0,3},{1,0},{2,1},{3,2},{4,7},{5,4},{6,5},{7,6},{8,11},{9,8},{10,9... | collective-permute-start | bytes 786440 | tf_op jit(solution)/shard_map/ppermute | solution.py:22
  387.6 7.5 %collective-permute-start.9 = (bf16[64,2048]{1,0:T(8,128)(2,1)S(1)}, bf16[64,2048]{1,0:T(8,128)(2,1)S(1)}, u32[]{:S(2)}, u32[]{:S(2)}) collective-permute-start(bf16[64,2048]{1,0:T(8,128)(2,1)S(1)} %collective-permute-done.8), channel_id=1, source_target_pairs={{0,1},{1,2},{2,3},{3,0},{4,5},{5,6},{6,7},{7,4},{8,9},{9,10},{10,1... | collective-permute-start | bytes 786440 | tf_op jit(solution)/shard_map/ppermute | solution.py:20
  (26 other events, 50.9 us)
Sparse Core Ops, SparseCore 0:
  144.4 21.2 reduce-scatter.4
  252.2 23.8 reduce-scatter.6
  355.0 23.9 reduce-scatter.8
  383.7 218.0 reduce-scatter.10
